TPU v7x, 512 devices: a whole 4x8x8 slice. The times are simulated.
512 devices in a mesh: layer: 16 (over x, z_hi, core), col: 32 (over z_lo, y).
Axes of the slice: x: 4, y: 8, z: 8 (z_hi: 2, z_lo: 4; z = z_hi * 4 + z_lo), core: 2. Of those that a mesh axis runs over, the one named last changes fastest.
Arguments:
- lower_panel: bfloat16 [16, 4096, 768], P('layer', 'col'), may hold values from -0.109375 to 0.109375
- upper_panel: bfloat16 [16, 768, 4096], P('layer', None, 'col'), may hold values from -6 to 6
- diag_inverse: bfloat16 [16, 1, 768, 768], P('layer'), may hold values from -1 to 2, as said below
- pivot_inverse: bfloat16 [4, 128, 128], replicated, may hold values from -0.1 to 0.1, as said below
- pattern: int32 [16, 2, 32], P('layer'), may hold values 0 or 1
- col_order: int32 [32], replicated, may hold values from 0 to 31, each once
- sep_blocks: int32 [4], replicated, may hold values from 0 to 31, as said below
Outputs:
- schur_top: bfloat16 [4096, 4096], P('layer', 'col')
Inputs may be any that keep to these rules, and one draw needn't show every extreme that they name: `diag_inverse`: each is the identity plus a full matrix of smaller entries. `pivot_inverse`: full matrices. `sep_blocks`: the 4 entries are distinct.
All inputs are finite; a program needn't handle non-finite values. No bound on the sum of `pattern` on one device may be relied on, other than what follows from the above.
Results may differ from a plain program's by a relative error of at most 0.0088.
Values may be sent and summed in bfloat16 or wider, within the bound.
No kernel may reach another device: no remote copies, remote signals or barrier semaphores. Data moves between devices by JAX's collectives and lax.ppermute only.
A program may use at most 64 MiB of HBM per device.

v0:
```python
import jax
import jax.numpy as jnp
from jax import lax
from jax.sharding import PartitionSpec as P

NB = 128


def from_partner(value, axis, distance):
    mask = 2**distance
    pairs = [(source, source ^ mask) for source in range(lax.axis_size(axis))]
    return lax.ppermute(value, axis, pairs)


def broadcast(x, axis, root):
    mine = lax.axis_index(axis) == root
    return lax.psum(jnp.where(mine, x, jnp.zeros_like(x)), axis)


def shards(lower_panel, upper_panel, diag_inverse, pivot_inverse, pattern, col_order, sep_blocks):
    supernodes = diag_inverse.shape[1]
    node_width = diag_inverse.shape[2]
    local_cols = upper_panel.shape[2]
    col_index = lax.axis_index("col")
    first_col = col_index * local_cols
    nblocks = col_order.shape[0]
    solved = jnp.einsum(
        "sab,sbc->sac",
        diag_inverse[0],
        upper_panel[0].reshape(supernodes, node_width, local_cols),
        preferred_element_type=jnp.float32,
    )
    right = solved.astype(jnp.bfloat16).reshape(supernodes * node_width, local_cols)
    row_flags = jnp.repeat(pattern[0, 0], NB).astype(jnp.float32)
    all_col_flags = jnp.repeat(pattern[0, 1], NB).astype(jnp.float32)
    col_flags = lax.dynamic_slice_in_dim(all_col_flags, first_col, local_cols)
    product = jnp.dot(
        lax.all_gather(lower_panel[0], "col", axis=0, tiled=True),
        right,
        preferred_element_type=jnp.float32,
    )
    current = (-product * row_flags[:, None] * col_flags[None, :]).astype(jnp.bfloat16)
    layer_count = lax.axis_size("layer")
    layer_index = lax.axis_index("layer")
    levels = layer_count.bit_length() - 1
    positions = jnp.arange(nblocks, dtype=jnp.int32)
    total_rows = current.shape[0]
    span_rows = total_rows // layer_count
    row_blocks = jnp.arange(total_rows, dtype=jnp.int32) // NB
    col_blocks = (first_col + jnp.arange(local_cols, dtype=jnp.int32)) // NB
    for level in range(levels):
        partner = from_partner(current, "layer", level)
        total = current.astype(jnp.float32) + partner.astype(jnp.float32)
        separator = sep_blocks[level]
        position = jnp.sum(jnp.where(col_order == separator, positions, 0))
        owner = position * NB // local_cols
        local_panel = total.astype(jnp.bfloat16)
        local_factor = jnp.dot(
            local_panel, pivot_inverse[level], preferred_element_type=jnp.float32
        ).astype(jnp.bfloat16)
        factor = broadcast(local_factor, "col", owner)
        upper_rows = lax.dynamic_slice_in_dim(total, separator * NB, NB, 0).astype(jnp.bfloat16)
        updated = total - jnp.dot(factor, upper_rows, preferred_element_type=jnp.float32)
        keep = (row_blocks != separator)[:, None] & (col_blocks != position)[None, :]
        current = jnp.where(keep, updated, jnp.zeros_like(updated)).astype(jnp.bfloat16)
    result = lax.dynamic_slice_in_dim(current, layer_index * span_rows, span_rows, 0)
    return result


def solution(mesh):
    in_specs = (
        P("layer", "col", None),
        P("layer", None, "col"),
        P("layer", None, None, None),
        P(),
        P("layer", None, None),
        P(),
        P(),
    )
    out_specs = P("layer", "col")
    return jax.shard_map(shards, mesh=mesh, in_specs=in_specs, out_specs=out_specs, check_vma=False)
```

profile of v0, /device:TPU:2, one launch (start us, length us, event | category | flops | bytes accessed | tf_op | source)
XLA Modules:
  0.0 1500.4 jit_solution(14784830018632039994)
XLA Ops:
  6.5 0.0 copy-start
  6.5 0.0 all-gather.3.cloned.1.call-start
  6.5 0.7 all-gather.3.cloned.1.call-update
  7.3 0.0 all-reduce.5.cloned.1.call-start
  7.3 0.8 convert_bitcast_fusion.1
  8.1 0.1 broadcast_bitcast_fusion
  8.1 0.1 dynamic_slice.18
  8.2 170.0 %all-gather.3.cloned.1.call-done = bf16[1,4096,768]{2,1,0:T(8,128)(2,1)} async-done(((bf16[1,128,768]{2,1,0:T(8,128)(2,1)}), bf16[1,4096,768]{2,1,0:T(8,128)(2,1)}) %all-gather.3.cloned.1.call-update) | async-done | bytes 6291472 | tf_op jit(solution)/shard_map/all_gather | solution.py:38
  178.2 0.0 copy-done
  178.2 0.0 copy-start.2
  178.2 0.0 copy-start.3
  178.2 0.0 copy-start.1
  178.2 5.8 fusion.24
  184.0 1.9 collective-permute-start
  185.9 0.0 copy-done.2
  185.9 0.6 fusion.66
  186.6 0.0 copy-done.3
  186.6 3.1 fusion.63
  190.3 0.6 fusion.53
  190.9 0.0 collective-permute-done
  191.0 0.0 copy-done.1
  191.0 1.6 fusion.20
  192.5 0.0 all-reduce.5.cloned.1.call-update
  192.6 0.0 all-reduce.7.cloned.1.call-start
  192.6 0.6 broadcast_compare_fusion
  193.9 1.6 convert_add_fusion.3
  195.5 304.2 %all-reduce.5.cloned.1.call-done = bf16[4096,128]{1,0:T(8,128)(2,1)} async-done(((bf16[4096,128]{1,0:T(8,128)(2,1)}), bf16[4096,128]{1,0:T(8,128)(2,1)}) %all-reduce.5.cloned.1.call-update) | async-done | bytes 1048592 | tf_op jit(solution)/shard_map/psum | solution.py:17
  499.7 2.4 fusion.17
  502.1 5.7 collective-permute-start.1
  508.4 0.7 fusion.54
  509.1 15.5 %collective-permute-done.1 = bf16[4096,128]{0,1:T(8,128)(2,1)S(1)} collective-permute-done((bf16[4096,128]{0,1:T(8,128)(2,1)S(1)}, bf16[4096,128]{0,1:T(8,128)(2,1)S(1)}, u32[]{:S(2)}, u32[]{:S(2)}) %collective-permute-start.1) | collective-permute-done | bytes 1048608 | tf_op jit(solution)/shard_map/ppermute | solution.py:12
  524.6 1.6 fusion.21
  526.2 0.0 all-reduce.7.cloned.1.call-update
  526.2 0.0 all-reduce.9.cloned.1.call-start
  526.3 0.6 broadcast_compare_fusion.1
  527.5 1.6 convert_add_fusion.2
  529.1 304.9 %all-reduce.7.cloned.1.call-done = bf16[4096,128]{1,0:T(8,128)(2,1)} async-done(((bf16[4096,128]{1,0:T(8,128)(2,1)}), bf16[4096,128]{1,0:T(8,128)(2,1)}) %all-reduce.7.cloned.1.call-update) | async-done | bytes 1048592 | tf_op jit(solution)/shard_map/psum | solution.py:17
  834.1 2.4 fusion.18
  836.5 2.5 collective-permute-start.2
  839.6 0.6 fusion.55
  840.2 13.0 collective-permute-done.2
  853.2 1.6 fusion.22
  854.8 0.0 all-reduce.9.cloned.1.call-update
  854.8 0.0 all-reduce.11.cloned.1.call-start
  854.9 0.6 broadcast_compare_fusion.2
  856.1 1.6 convert_add_fusion.1
  857.7 303.8 %all-reduce.9.cloned.1.call-done = bf16[4096,128]{1,0:T(8,128)(2,1)} async-done(((bf16[4096,128]{1,0:T(8,128)(2,1)}), bf16[4096,128]{1,0:T(8,128)(2,1)}) %all-reduce.9.cloned.1.call-update) | async-done | bytes 1048592 | tf_op jit(solution)/shard_map/psum | solution.py:17
  1161.5 2.4 fusion.19
  1163.9 4.0 collective-permute-start.3
  1168.6 0.6 fusion.56
  1169.2 12.9 collective-permute-done.3
  1182.1 1.6 fusion.23
  1183.7 0.0 all-reduce.11.cloned.1.call-update
  1183.7 0.7 broadcast_compare_fusion.3
  1185.0 0.1 dynamic-slice
  1185.1 1.6 convert_add_fusion
  1186.7 303.8 %all-reduce.11.cloned.1.call-done = bf16[4096,128]{1,0:T(8,128)(2,1)} async-done(((bf16[4096,128]{1,0:T(8,128)(2,1)}), bf16[4096,128]{1,0:T(8,128)(2,1)}) %all-reduce.11.cloned.1.call-update) | async-done | bytes 1048592 | tf_op jit(solution)/shard_map/psum | solution.py:17
  1490.4 1.7 fusion.42
  1492.1 1.0 fusion.41
  1493.1 0.7 copy.12
Async XLA Ops:
  6.5 171.7 %copy-start = (bf16[1,1,768,768]{3,2,1,0:T(8,128)(2,1)S(1)}, bf16[1,1,768,768]{3,2,1,0:T(8,128)(2,1)}, u32[]{:S(2)}) copy-start(bf16[1,1,768,768]{3,2,1,0:T(8,128)(2,1)} %param.9) | copy-start | bytes 3538948
  6.5 171.6 %all-gather.3.cloned.1.call-start = ((), (), s32[]{:S(2)}) async-start(), calls=%async_computation.4 | async-start | bytes 6488064 | tf_op jit(solution)/shard_map/all_gather | solution.py:38
  7.3 492.4 %all-reduce.5.cloned.1.call-start = ((), (), s32[]{:S(2)}) async-start(), calls=%async_computation | async-start | bytes 2097152 | tf_op jit(solution)/shard_map/psum | solution.py:17
  178.2 7.7 copy-start.2
  178.2 8.4 copy-start.3
  178.2 12.8 copy-start.1
  184.0 6.9 collective-permute-start
  192.6 641.5 %all-reduce.7.cloned.1.call-start = ((), (), s32[]{:S(2)}) async-start(), calls=%async_computation.1 | async-start | bytes 2097152 | tf_op jit(solution)/shard_map/psum | solution.py:17
  502.1 22.5 %collective-permute-start.1 = (bf16[4096,128]{0,1:T(8,128)(2,1)S(1)}, bf16[4096,128]{0,1:T(8,128)(2,1)S(1)}, u32[]{:S(2)}, u32[]{:S(2)}) collective-permute-start(bf16[4096,128]{0,1:T(8,128)(2,1)S(1)} %fusion.17), channel_id=1, source_target_pairs={{0,64},{32,96},{64,0},{96,32},{128,192},{160,224},{192,128},{224,1... | collective-permute-start | bytes 3145736 | tf_op jit(solution)/shard_map/ppermute | solution.py:12
  526.2 635.3 %all-reduce.9.cloned.1.call-start = ((), (), s32[]{:S(2)}) async-start(), calls=%async_computation.2 | async-start | bytes 2097152 | tf_op jit(solution)/shard_map/psum | solution.py:17
  836.5 16.7 %collective-permute-start.2 = (bf16[4096,128]{0,1:T(8,128)(2,1)S(1)}, bf16[4096,128]{0,1:T(8,128)(2,1)S(1)}, u32[]{:S(2)}, u32[]{:S(2)}) collective-permute-start(bf16[4096,128]{0,1:T(8,128)(2,1)S(1)} %fusion.18), channel_id=1, source_target_pairs={{0,128},{32,160},{64,192},{96,224},{128,0},{160,32},{192,64},{224,... | collective-permute-start | bytes 3145736 | tf_op jit(solution)/shard_map/ppermute | solution.py:12
  854.8 635.6 %all-reduce.11.cloned.1.call-start = ((), (), s32[]{:S(2)}) async-start(), calls=%async_computation.3 | async-start | bytes 2097152 | tf_op jit(solution)/shard_map/psum | solution.py:17
  1163.9 18.2 %collective-permute-start.3 = (bf16[4096,128]{0,1:T(8,128)(2,1)S(1)}, bf16[4096,128]{0,1:T(8,128)(2,1)S(1)}, u32[]{:S(2)}, u32[]{:S(2)}) collective-permute-start(bf16[4096,128]{0,1:T(8,128)(2,1)S(1)} %fusion.19), channel_id=1, source_target_pairs={{0,256},{32,288},{64,320},{96,352},{128,384},{160,416},{192,448},{... | collective-permute-start | bytes 3145736 | tf_op jit(solution)/shard_map/ppermute | solution.py:12
Sparse Core Ops, SparseCore 0:
  9.4 168.7 all-gather.2
  192.7 306.9 all-reduce.4
  526.3 307.6 all-reduce.6
  854.9 306.5 all-reduce.8
  1183.8 306.5 all-reduce.10
where the time goes:
time: 1500 us
  waiting for transfers between devices  1430 us (95%)
  matrix products  21 us (1%)
  between operations  18.4 us (1%)
  other arithmetic  16.3 us (1%)
    psum x4, waiting for transfers between devices, broadcast(): return lax.psum(jnp.where(mine, x, jnp.zeros_like(x)), axis)  1220 us
    all_gather x1, waiting for transfers between devices, shards(): lax.all_gather(lower_panel[0], 'col', axis=0, tiled=True)  170 us
    ppermute x4, waiting for transfers between devices, from_partner(): return lax.ppermute(value, axis, pairs)  41.4 us
  transfers between devices with their start and end apart: 9, of which 8 were waited for; matrix products, arithmetic and copies ran while one was open for 1% of the time, Pallas kernels for 0%

commit v1 on v0

--- a/solution.py
+++ b/solution.py
@@ -14,7 +14,7 @@
 
 def broadcast(x, axis, root):
     mine = lax.axis_index(axis) == root
-    return lax.psum(jnp.where(mine, x, jnp.zeros_like(x)), axis)
+    return jnp.sum(lax.all_gather(jnp.where(mine, x, jnp.zeros_like(x)), axis), axis=0)
 
 
 def shards(lower_panel, upper_panel, diag_inverse, pivot_inverse, pattern, col_order, sep_blocks):

time: 1500 us -> 1830 us (1.22)
  the two profiles are of different devices: /device:TPU:2 before, /device:TPU:1 now
where the time goes in v1:
time: 1830 us
  waiting for transfers between devices  1690 us (92%)
  other arithmetic  64.7 us (4%)
  starting transfers between devices  36 us (2%)
  matrix products  18.4 us (1%)
    all_gather x4, waiting for transfers between devices, broadcast(): lax.all_gather(jnp.where(mine, x, jnp.zeros_like(x)), axis)  1450 us
    all_gather x1, waiting for transfers between devices, shards(): lax.all_gather(lower_panel[0], 'col', axis=0, tiled=True)  150 us
    ppermute x4, waiting for transfers between devices, from_partner(): return lax.ppermute(value, axis, pairs)  90.9 us
    reduce_sum x4, other arithmetic, broadcast(): jnp.sum(lax.all_gather(jnp.where(mine, x, jnp.zeros_like(x)), axis), axis=0)  48.8 us
  transfers between devices with their start and end apart: 9, of which 8 were waited for; matrix products, arithmetic and copies ran while one was open for 1% of the time, Pallas kernels for 0%

profile of v1, /device:TPU:1, one launch (start us, length us, event | category | flops | bytes accessed | tf_op | source)
XLA Modules:
  0.0 1833.0 jit_solution(11210634963639540400)
XLA Ops:
  6.5 0.0 copy-start
  6.5 0.0 all-gather.11.cloned.1.call-start
  6.5 0.7 all-gather.11.cloned.1.call-update
  7.3 0.0 all-gather.13.cloned.1.call-start
  7.3 0.8 convert_bitcast_fusion.1
  8.1 0.1 broadcast_bitcast_fusion
  8.1 0.1 dynamic_slice.18
  8.2 150.3 %all-gather.11.cloned.1.call-done = bf16[1,4096,768]{2,1,0:T(8,128)(2,1)} async-done(((bf16[1,128,768]{2,1,0:T(8,128)(2,1)}), bf16[1,4096,768]{2,1,0:T(8,128)(2,1)}) %all-gather.11.cloned.1.call-update) | async-done | bytes 6291472 | tf_op jit(solution)/shard_map/all_gather | solution.py:38
  158.5 0.0 copy-done
  158.5 5.8 fusion.24
  164.3 23.1 %collective-permute-start = (bf16[4096,128]{0,1:T(8,128)(2,1)S(1)}, bf16[4096,128]{0,1:T(8,128)(2,1)S(1)}, u32[]{:S(2)}, u32[]{:S(2)}) collective-permute-start(bf16[4096,128]{0,1:T(8,128)(2,1)S(1)} %fusion.24), channel_id=1, source_target_pairs={{0,32},{32,0},{64,96},{96,64},{128,160},{160,128},{192,224},{224,1... | collective-permute-start | bytes 3145736 | tf_op jit(solution)/shard_map/ppermute | solution.py:12
  187.4 0.0 copy-done.6
  187.4 0.7 fusion.66
  188.1 0.0 copy-done.7
  188.1 3.2 fusion.63
  191.9 0.0 collective-permute-done
  191.9 0.0 copy-done.5
  191.9 1.5 fusion.20
  193.4 0.0 all-gather.13.cloned.1.call-update
  193.5 0.0 all-gather.15.cloned.1.call-start
  194.1 0.6 broadcast_compare_fusion
  194.7 0.6 fusion.53
  195.3 1.6 convert_add_fusion.3
  196.8 361.3 %all-gather.13.cloned.1.call-done = bf16[131072,128]{1,0:T(8,128)(2,1)} async-done(((bf16[4096,128]{1,0:T(8,128)(2,1)}), bf16[131072,128]{1,0:T(8,128)(2,1)}) %all-gather.13.cloned.1.call-update) | async-done | bytes 33554448 | tf_op jit(solution)/shard_map/all_gather | solution.py:17
  558.1 12.5 reduce_sum.88
  570.6 0.0 copy-done.2
  570.6 1.7 fusion.17
  572.4 5.0 collective-permute-start.1
  578.0 46.8 %collective-permute-done.1 = bf16[4096,128]{0,1:T(8,128)(2,1)S(1)} collective-permute-done((bf16[4096,128]{0,1:T(8,128)(2,1)S(1)}, bf16[4096,128]{0,1:T(8,128)(2,1)S(1)}, u32[]{:S(2)}, u32[]{:S(2)}) %collective-permute-start.1) | collective-permute-done | bytes 1048608 | tf_op jit(solution)/shard_map/ppermute | solution.py:12
  624.7 1.6 fusion.21
  626.3 0.0 all-gather.15.cloned.1.call-update
  626.3 0.0 copy-done.3
  626.3 0.0 all-gather.17.cloned.1.call-start
  627.0 0.6 broadcast_compare_fusion.1
  627.6 0.7 fusion.54
  628.3 1.5 convert_add_fusion.2
  629.8 363.6 %all-gather.15.cloned.1.call-done = bf16[131072,128]{1,0:T(8,128)(2,1)} async-done(((bf16[4096,128]{1,0:T(8,128)(2,1)}), bf16[131072,128]{1,0:T(8,128)(2,1)}) %all-gather.15.cloned.1.call-update) | async-done | bytes 33554448 | tf_op jit(solution)/shard_map/all_gather | solution.py:17
  993.3 12.4 reduce_sum.89
  1005.7 1.7 fusion.18
  1007.4 3.1 collective-permute-start.2
  1011.1 22.1 %collective-permute-done.2 = bf16[4096,128]{0,1:T(8,128)(2,1)S(1)} collective-permute-done((bf16[4096,128]{0,1:T(8,128)(2,1)S(1)}, bf16[4096,128]{0,1:T(8,128)(2,1)S(1)}, u32[]{:S(2)}, u32[]{:S(2)}) %collective-permute-start.2) | collective-permute-done | bytes 1048608 | tf_op jit(solution)/shard_map/ppermute | solution.py:12
  1033.2 1.6 fusion.22
  1034.8 0.0 all-gather.17.cloned.1.call-update
  1034.8 0.0 all-gather.19.cloned.1.call-start
  1035.5 0.6 broadcast_compare_fusion.2
  1036.1 0.7 fusion.55
  1036.8 1.5 convert_add_fusion.1
  1038.3 363.6 %all-gather.17.cloned.1.call-done = bf16[131072,128]{1,0:T(8,128)(2,1)} async-done(((bf16[4096,128]{1,0:T(8,128)(2,1)}), bf16[131072,128]{1,0:T(8,128)(2,1)}) %all-gather.17.cloned.1.call-update) | async-done | bytes 33554448 | tf_op jit(solution)/shard_map/all_gather | solution.py:17
  1401.9 12.4 reduce_sum.90
  1414.3 1.7 fusion.19
  1416.0 4.6 collective-permute-start.3
  1421.2 22.1 %collective-permute-done.3 = bf16[4096,128]{0,1:T(8,128)(2,1)S(1)} collective-permute-done((bf16[4096,128]{0,1:T(8,128)(2,1)S(1)}, bf16[4096,128]{0,1:T(8,128)(2,1)S(1)}, u32[]{:S(2)}, u32[]{:S(2)}) %collective-permute-start.3) | collective-permute-done | bytes 1048608 | tf_op jit(solution)/shard_map/ppermute | solution.py:12
  1443.3 1.5 fusion.23
  1444.8 0.0 all-gather.19.cloned.1.call-update
  1445.5 0.6 fusion.56
  1446.1 0.1 dynamic-slice
  1446.2 0.6 broadcast_compare_fusion.3
  1446.7 1.6 convert_add_fusion
  1448.3 363.6 %all-gather.19.cloned.1.call-done = bf16[131072,128]{1,0:T(8,128)(2,1)} async-done(((bf16[4096,128]{1,0:T(8,128)(2,1)}), bf16[131072,128]{1,0:T(8,128)(2,1)}) %all-gather.19.cloned.1.call-update) | async-done | bytes 33554448 | tf_op jit(solution)/shard_map/all_gather | solution.py:17
  1811.9 11.5 reduce_sum.91
  1823.4 1.3 fusion.42
  1824.7 1.0 fusion.41
  1825.7 0.7 copy.12
  1826.4 0.0 copy-done.1
  (8 shorter events, 0.0 us)
Async XLA Ops:
  6.5 152.0 %copy-start = (bf16[1,1,768,768]{3,2,1,0:T(8,128)(2,1)S(1)}, bf16[1,1,768,768]{3,2,1,0:T(8,128)(2,1)}, u32[]{:S(2)}) copy-start(bf16[1,1,768,768]{3,2,1,0:T(8,128)(2,1)} %param.9) | copy-start | bytes 3538948
  6.5 152.0 %all-gather.11.cloned.1.call-start = ((), (), s32[]{:S(2)}) async-start(), calls=%async_computation | async-start | bytes 6488064 | tf_op jit(solution)/shard_map/all_gather | solution.py:38
  7.3 550.9 %all-gather.13.cloned.1.call-start = ((), (), s32[]{:S(2)}) async-start(), calls=%async_computation.1 | async-start | bytes 34603008 | tf_op jit(solution)/shard_map/all_gather | solution.py:17
  158.5 28.9 %copy-start.6 = (s32[4]{0:T(128)S(1)}, s32[4]{0:T(128)}, u32[]{:S(2)}) copy-start(s32[4]{0:T(128)} %param.13) | copy-start | bytes 52
  158.5 29.6 %copy-start.7 = (s32[32]{0:T(128)S(1)}, s32[32]{0:T(128)}, u32[]{:S(2)}) copy-start(s32[32]{0:T(128)} %param.12) | copy-start | bytes 388
  158.5 33.4 %copy-start.5 = (bf16[4,128,128]{2,1,0:T(8,128)(2,1)S(1)}, bf16[4,128,128]{2,1,0:T(8,128)(2,1)}, u32[]{:S(2)}) copy-start(bf16[4,128,128]{2,1,0:T(8,128)(2,1)} %param.10) | copy-start | bytes 393220
  164.3 27.6 %collective-permute-start = (bf16[4096,128]{0,1:T(8,128)(2,1)S(1)}, bf16[4096,128]{0,1:T(8,128)(2,1)S(1)}, u32[]{:S(2)}, u32[]{:S(2)}) collective-permute-start(bf16[4096,128]{0,1:T(8,128)(2,1)S(1)} %fusion.24), channel_id=1, source_target_pairs={{0,32},{32,0},{64,96},{96,64},{128,160},{160,128},{192,224},{224,1... | collective-permute-start | bytes 3145736 | tf_op jit(solution)/shard_map/ppermute | solution.py:12
  193.5 799.8 %all-gather.15.cloned.1.call-start = ((), (), s32[]{:S(2)}) async-start(), calls=%async_computation.2 | async-start | bytes 34603008 | tf_op jit(solution)/shard_map/all_gather | solution.py:17
  558.1 12.5 copy-start.2
  572.4 52.4 %collective-permute-start.1 = (bf16[4096,128]{0,1:T(8,128)(2,1)S(1)}, bf16[4096,128]{0,1:T(8,128)(2,1)S(1)}, u32[]{:S(2)}, u32[]{:S(2)}) collective-permute-start(bf16[4096,128]{0,1:T(8,128)(2,1)S(1)} %fusion.17), channel_id=1, source_target_pairs={{0,64},{32,96},{64,0},{96,32},{128,192},{160,224},{192,128},{224,1... | collective-permute-start | bytes 3145736 | tf_op jit(solution)/shard_map/ppermute | solution.py:12
  624.7 1.6 copy-start.3
  626.3 775.5 %all-gather.17.cloned.1.call-start = ((), (), s32[]{:S(2)}) async-start(), calls=%async_computation.3 | async-start | bytes 34603008 | tf_op jit(solution)/shard_map/all_gather | solution.py:17
  1007.4 25.8 %collective-permute-start.2 = (bf16[4096,128]{0,1:T(8,128)(2,1)S(1)}, bf16[4096,128]{0,1:T(8,128)(2,1)S(1)}, u32[]{:S(2)}, u32[]{:S(2)}) collective-permute-start(bf16[4096,128]{0,1:T(8,128)(2,1)S(1)} %fusion.18), channel_id=1, source_target_pairs={{0,128},{32,160},{64,192},{96,224},{128,0},{160,32},{192,64},{224,... | collective-permute-start | bytes 3145736 | tf_op jit(solution)/shard_map/ppermute | solution.py:12
  1033.2 1.6 copy-start.4
  1034.8 777.1 %all-gather.19.cloned.1.call-start = ((), (), s32[]{:S(2)}) async-start(), calls=%async_computation.4 | async-start | bytes 34603008 | tf_op jit(solution)/shard_map/all_gather | solution.py:17
  1416.0 27.3 %collective-permute-start.3 = (bf16[4096,128]{0,1:T(8,128)(2,1)S(1)}, bf16[4096,128]{0,1:T(8,128)(2,1)S(1)}, u32[]{:S(2)}, u32[]{:S(2)}) collective-permute-start(bf16[4096,128]{0,1:T(8,128)(2,1)S(1)} %fusion.19), channel_id=1, source_target_pairs={{0,256},{32,288},{64,320},{96,352},{128,384},{160,416},{192,448},{... | collective-permute-start | bytes 3145736 | tf_op jit(solution)/shard_map/ppermute | solution.py:12
  1811.9 14.5 copy-start.1
Sparse Core Ops, SparseCore 0:
  9.4 149.0 all-gather.10
  193.6 364.5 all-gather.12
  626.5 366.8 all-gather.14
  1034.9 366.9 all-gather.16
  1444.9 366.9 all-gather.18
